TPU v7x, 32 devices: a whole 2x2x4 slice. The times are simulated.
32 devices in a mesh: row: 4 (over x, core), col: 8 (over z, y).
Axes of the slice: x: 2, y: 2, z: 4, core: 2. Of those that a mesh axis runs over, the one named last changes fastest.
Arguments:
- velocity: float32 [3, 16, 2048, 1024], P(None, None, 'col', 'row'), may hold values from -6 to 6
- z_inverse: float32 [1024, 1024], replicated, may hold values from -0.1875 to 0.1875
- tiles: int32 [256, 4], P(('row', 'col')), may hold values from 0 to 4095, as said below
- amplitude: float32 [256, 4, 256], P(('row', 'col')), may hold values from -3 to 3
- lateral: float32 [256, 8, 256], P(('row', 'col')), may hold values from -2 to 2
- vertical: float32 [256, 256, 256], P(('row', 'col')), may hold values from -0.375 to 0.375
- wall_velocity: float32 [256, 3, 256], P(('row', 'col')), may hold values from -6 to 6
- surface: float32 [256, 256], P(('row', 'col')), may hold values from 0.5 to 2
Outputs:
- spectrum: float32 [2, 3, 16, 1024, 1024], P(None, None, 'row', 'col')
- marker_force: float32 [256, 3, 256], P(('row', 'col'))
Inputs may be any that keep to these rules, and one draw needn't show every extreme that they name: tiles[b, k] is a tile id in block b's row group; the column index holding tile t is t // 512. Among the 32 entries of one device's blocks, at most 8 (repeats counted) name tiles held by one column index.
All inputs are finite; a program needn't handle non-finite values.
Results may differ from a plain program's by a relative error of at most 0.000071.
Values sent between devices are 32-bit elements; how exact they have to be, the bound alone decides.
No kernel may reach another device: no remote copies, remote signals or barrier semaphores. Data moves between devices by JAX's collectives and lax.ppermute only.
A program may use at most 128 MiB of HBM per device.

v0:
```python
import jax
import jax.numpy as jnp
from jax import lax
from jax.sharding import PartitionSpec as P

NY = 2048
TY = 8
K = 4
CAP = 8


smoothing = 1.0


def tile_slots(requests, tile_count, columns):
    holder = requests // tile_count
    within = requests % tile_count
    hits = (holder[:, None] == jnp.arange(columns, dtype=jnp.int32)[None, :]).astype(jnp.int32)
    before = jnp.cumsum(hits, axis=0) - hits
    place = jnp.sum(before * hits, axis=1)
    return (holder, within, place)


def local(velocity, z_inverse, tiles, amplitude, lateral, vertical, wall_velocity, surface):
    width_x = velocity.shape[1]
    rows_y = velocity.shape[2]
    depth = velocity.shape[3]
    columns = lax.axis_size("col")
    per_row = rows_y // TY
    tile_count = width_x * per_row
    blocks = tiles.shape[0]
    requests = tiles.reshape(-1)
    request_count = requests.shape[0]
    holder, within, place = tile_slots(requests, tile_count, columns)
    target_slot = holder * CAP + place
    wanted = (
        jnp.zeros((columns * CAP,), jnp.int32).at[target_slot].set(within).reshape(columns, CAP)
    )
    served = lax.all_to_all(wanted, "col", split_axis=0, concat_axis=0, tiled=True)
    store = (
        velocity.reshape(3, width_x, per_row, TY, depth)
        .transpose(1, 2, 0, 3, 4)
        .reshape(tile_count, 3, TY, depth)
    )
    served_flat = served.reshape(-1)
    outgoing_tiles = store[served_flat].reshape(columns, CAP, 3, TY, depth)
    fetched = lax.all_to_all(
        outgoing_tiles, "col", split_axis=0, concat_axis=0, tiled=True
    ).reshape(columns * CAP, 3, TY, depth)
    mine = fetched[target_slot].reshape(blocks, K, 3, TY, depth)
    inner = jnp.einsum("bkcyz,bzi->bkcyi", mine, vertical, precision=lax.Precision.HIGHEST)
    weight = amplitude[:, :, None, :] * lateral[:, None, :, :]
    sampled = jnp.sum(weight[:, :, None] * inner, axis=(1, 3))
    marker_force = wall_velocity - sampled
    share = weight[:, :, None] * (surface[:, None, :] * marker_force)[:, None, :, None, :]
    spread = jnp.einsum("bkcyi,bzi->bkcyz", share, vertical, precision=lax.Precision.HIGHEST)
    spread = spread.reshape(request_count, 3, TY, depth)
    outgoing = jnp.zeros((columns * CAP, 3, TY, depth), jnp.float32).at[target_slot].set(spread)
    incoming = lax.all_to_all(
        outgoing.reshape(columns, CAP, 3, TY, depth), "col", split_axis=0, concat_axis=0, tiled=True
    )
    forced_store = store.at[served_flat].add(incoming.reshape(columns * CAP, 3, TY, depth))
    forced = (
        forced_store.reshape(width_x, per_row, 3, TY, depth)
        .transpose(2, 0, 1, 3, 4)
        .reshape(3, width_x, rows_y, depth)
    )
    depthwise = jnp.einsum(
        "cxyz,zw->xcwy",
        lax.all_to_all(forced, "row", split_axis=1, concat_axis=3, tiled=True),
        z_inverse,
        precision=lax.Precision.HIGHEST,
    )
    places = jnp.arange(NY, dtype=jnp.int32)
    wavenumber = jnp.arange(NY // 2, dtype=jnp.int32)
    phase = (places[:, None] * wavenumber[None, :] % NY).astype(jnp.float32) * (2.0 * jnp.pi / NY)
    wave = wavenumber.astype(jnp.float32)
    damping = (
        1.0 / (1.0 + 4.0 * smoothing * jnp.sin(jnp.pi * wave / NY) ** 2) / jnp.sqrt(jnp.float32(NY))
    )
    table = jnp.stack(
        [jnp.cos(phase) * damping[None, :], -jnp.sin(phase) * damping[None, :]], axis=1
    )
    spectrum = jnp.einsum(
        "xczy,ypk->pcxzk",
        lax.all_to_all(depthwise, "col", split_axis=2, concat_axis=3, tiled=True),
        table,
        precision=lax.Precision.HIGHEST,
    )
    return (spectrum, marker_force)


def solution(mesh):
    in_specs = (
        P(None, None, "col", "row"),
        P(),
        P(("row", "col"), None),
        P(("row", "col"), None, None),
        P(("row", "col"), None, None),
        P(("row", "col"), None, None),
        P(("row", "col"), None, None),
        P(("row", "col"), None),
    )
    out_specs = (P(None, None, "row", "col", None), P(("row", "col"), None, None))
    return jax.shard_map(local, mesh=mesh, in_specs=in_specs, out_specs=out_specs, check_vma=False)
```

profile of v0, /device:TPU:0, one launch (start us, length us, event | category | flops | bytes accessed | tf_op | source)
XLA Modules:
  0.0 780.4 jit_solution(209504987380438527)
XLA Ops:
  3.4 7.3 all-to-all-start
  10.7 10.6 %copy.23 = f32[3,16,32,8,256]{4,3,0,2,1:T(8,128)} copy(f32[3,16,32,8,256]{4,3,2,1,0:T(8,128)} %bitcast.76) | data formatting | bytes 25165824 | tf_op jit(solution)/shard_map/reshape | solution.py:41
  22.6 6.4 gather_fusion
  29.0 6.0 all-to-all-start.1
  35.1 36.5 %all-to-all-done.1 = f32[8,8,3,8,256]{4,3,2,1,0:T(8,128)} async-done(((f32[8,8,3,8,256]{4,3,2,1,0:T(8,128)}), f32[8,8,3,8,256]{4,3,2,1,0:T(8,128)}, u32[]{:S(2)}, u32[]{:S(2)}) %all-to-all-start.1) | async-done | bytes 1572896 | tf_op jit(solution)/shard_map/all_to_all | solution.py:47
  71.6 2.0 gather_fusion.1
  73.6 1.4 fusion.18
  75.1 2.1 fusion.11
  77.2 1.7 scatter_fusion
  79.0 40.7 %all_to_all.55 = f32[8,8,3,8,256]{4,3,2,1,0:T(8,128)} all-to-all(f32[8,8,3,8,256]{4,3,2,1,0:T(8,128)S(1)} %bitcast.77), channel_id=1, replica_groups=mesh['row'=4,'col'=8] {'col'}, dimensions={0} | all-to-all | bytes 3145728 | tf_op jit(solution)/shard_map/all_to_all | solution.py:59
  119.7 10.0 %scatter_fusion.1 = f32[512,3,8,256]{3,2,1,0:T(8,128)} fusion(f32[512,3,8,256]{3,2,1,0:T(8,128)} %bitcast.71, s32[64]{0:T(128)S(1)} %fusion.26, f32[64,3,8,256]{3,2,1,0:T(8,128)} %bitcast.78), kind=kCustom, calls=%fused_computation.4 | custom fusion | flops 393216 | bytes 4718848 | tf_op jit(solution)/shard_map/scatter-add | solution.py:62
  129.6 10.8 %copy.44 = f32[3,16,32,8,256]{4,3,2,0,1:T(8,128)} copy(f32[3,16,32,8,256]{4,3,0,2,1:T(8,128)} %bitcast.72) | data formatting | bytes 25165824 | tf_op jit(solution)/shard_map/transpose | solution.py:65
  140.4 142.6 %all_to_all.56 = f32[3,16,256,256]{3,2,0,1:T(8,128)S(1)} all-to-all(f32[3,16,256,256]{3,2,0,1:T(8,128)} %bitcast.73), channel_id=1, replica_groups=mesh['row'=4,'col'=8] {'row'}, dimensions={1} | all-to-all | bytes 25165824 | tf_op jit(solution)/shard_map/all_to_all | solution.py:70
  283.0 8.9 %copy.30 = f32[3,4,256,4,256]{4,3,2,1,0:T(4,128)} copy(f32[3,4,256,4,256]{4,2,0,1,3:T(8,128)S(1)} %bitcast.74) | data formatting | bytes 25165824 | tf_op jit(solution)/shard_map/all_to_all | solution.py:70
  292.0 15.7 %all_to_all.45 = f32[3,4,256,1024]{3,2,1,0:T(8,128)} reshape(f32[3,4,256,4,256]{4,3,2,1,0:T(4,128)} %copy.30) | data formatting | bytes 25165824 | tf_op jit(solution)/shard_map/all_to_all | solution.py:70
  307.7 45.8 %convolution_bitcast_fusion = f32[4,3,1024,256]{2,3,0,1:T(8,128)} fusion(f32[3,4,256,1024]{3,2,1,0:T(8,128)} %all_to_all.45, f32[1024,1024]{1,0:T(8,128)} %param.9), kind=kOutput, calls=%fused_computation.23 | convolution fusion | flops 38654705664 | bytes 29360128 | tf_op jit(solution)/shard_map/cxyz,zw->xcwy/dot_general | solution.py:68
  353.4 14.7 %copy.31 = f32[4,3,1024,256]{3,0,1,2:T(4,128)} copy(f32[4,3,1024,256]{2,3,0,1:T(8,128)} %convolution_bitcast_fusion) | data formatting | bytes 25165824 | tf_op jit(solution)/shard_map/cxyz,zw->xcwy/transpose | solution.py:68
  368.1 5.6 all-to-all-start.4
  373.7 35.3 %cosine_multiply_fusion = (f32[2048,1,1024]{0,2,1:T(8,128)}, f32[2048,1,1024]{0,2,1:T(8,128)}) fusion(f32[1024]{0:T(1024)S(1)} %divide_multiply_fusion), kind=kLoop, calls=%fused_computation.18 | loop fusion | flops 35651584 | bytes 16781312 | tf_op jit(solution)/shard_map/mul | solution.py:82
  409.6 236.9 %all-to-all-done.4 = f32[4,3,1024,256]{3,0,1,2:T(4,128)} async-done(((f32[4,3,1024,256]{3,0,1,2:T(4,128)}), f32[4,3,1024,256]{3,0,1,2:T(4,128)}, u32[]{:S(2)}, u32[]{:S(2)}) %all-to-all-start.4) | async-done | bytes 12582944 | tf_op jit(solution)/shard_map/all_to_all | solution.py:86
  646.5 16.6 %copy.43 = f32[4,3,8,128,256]{4,2,3,1,0:T(8,128)} copy(f32[4,3,8,128,256]{4,0,1,3,2:T(4,128)} %bitcast.27) | data formatting | bytes 25165824 | tf_op jit(solution)/shard_map/all_to_all | solution.py:86
  663.2 13.6 %reshape.356 = f32[4,3,128,2048,1]{3,2,1,0,4:T(8,128)} reshape(f32[4,3,128,8,256]{4,3,2,1,0:T(8,128)} %bitcast.75) | data formatting | bytes 25165824 | tf_op jit(solution)/shard_map/all_to_all | solution.py:86
  676.8 90.5 %fusion.9 = f32[2,3,4,128,1024]{3,4,1,2,0:T(8,128)} fusion(f32[4,3,128,2048,1]{3,2,1,0,4:T(8,128)} %reshape.356, f32[2048,1,1024]{0,2,1:T(8,128)} %get-tuple-element.11, f32[2048,1,1024]{0,2,1:T(8,128)} %get-tuple-element.10), kind=kOutput, calls=%fused_computation.22 | convolution fusion | flops 77313605632 | bytes 41943040 | tf_op jit(solution)/shard_map/xczy,ypk->pcxzk/dot_general | solution.py:84
  767.3 12.6 %copy.33 = f32[2,3,4,128,1024]{4,3,2,1,0:T(8,128)} copy(f32[2,3,4,128,1024]{3,4,1,2,0:T(8,128)} %fusion.9) | data formatting | bytes 25165824
  (34 shorter events, 4.9 us)
Async XLA Ops:
  0.6 72.9 %copy-start = (f32[8,256,256]{2,1,0:T(8,128)S(1)}, f32[8,256,256]{2,1,0:T(8,128)}, u32[]{:S(2)}) copy-start(f32[8,256,256]{2,1,0:T(8,128)} %param.13) | copy-start | bytes 6291460
  3.4 18.0 %all-to-all-start = ((s32[8,1,8]{2,1,0:T(1,128)}), s32[8,1,8]{2,1,0:T(1,128)S(1)}, u32[]{:S(2)}, u32[]{:S(2)}) async-start(s32[8,1,8]{2,1,0:T(1,128)} %bitcast.7), calls=%async_computation | async-start | bytes 8192 | tf_op jit(solution)/shard_map/all_to_all | solution.py:39
  10.7 24.3 %copy-start.2 = (f32[8,8,256]{2,1,0:T(8,128)S(1)}, f32[8,8,256]{2,1,0:T(8,128)}, u32[]{:S(2)}) copy-start(f32[8,8,256]{2,1,0:T(8,128)} %param.12) | copy-start | bytes 196612
  10.7 24.3 %copy-start.3 = (f32[8,4,256]{2,1,0:T(4,128)S(1)}, f32[8,4,256]{2,1,0:T(4,128)}, u32[]{:S(2)}) copy-start(f32[8,4,256]{2,1,0:T(4,128)} %param.11) | copy-start | bytes 98308
  21.4 53.6 %copy-start.4 = (f32[8,3,256]{2,0,1:T(8,128)S(1)}, f32[8,3,256]{2,0,1:T(8,128)}, u32[]{:S(2)}) copy-start(f32[8,3,256]{2,0,1:T(8,128)} %param.14) | copy-start | bytes 73732
  21.4 53.6 %copy-start.5 = (f32[8,256]{1,0:T(8,128)S(1)}, f32[8,256]{1,0:T(8,128)}, u32[]{:S(2)}) copy-start(f32[8,256]{1,0:T(8,128)} %param.15) | copy-start | bytes 24580
  29.0 42.5 %all-to-all-start.1 = ((f32[8,8,3,8,256]{4,3,2,1,0:T(8,128)}), f32[8,8,3,8,256]{4,3,2,1,0:T(8,128)}, u32[]{:S(2)}, u32[]{:S(2)}) async-start(f32[8,8,3,8,256]{4,3,2,1,0:T(8,128)} %bitcast.79), calls=%async_computation.1 | async-start | bytes 3145728 | tf_op jit(solution)/shard_map/all_to_all | solution.py:47
  368.1 278.4 %all-to-all-start.4 = ((f32[4,3,1024,256]{3,0,1,2:T(4,128)}), f32[4,3,1024,256]{3,0,1,2:T(4,128)}, u32[]{:S(2)}, u32[]{:S(2)}) async-start(f32[4,3,1024,256]{3,0,1,2:T(4,128)} %copy.31), calls=%async_computation.4 | async-start | bytes 25165824 | tf_op jit(solution)/shard_map/all_to_all | solution.py:86
  676.8 103.2 %copy-start.1 = (f32[8,256,256]{2,1,0:T(8,128)S(1)}, f32[8,256,256]{2,1,0:T(8,128)}, u32[]{:S(2)}) copy-start(f32[8,256,256]{2,1,0:T(8,128)} %param.13) | copy-start | bytes 6291460
where the time goes:
time: 788 us; the launch traced here: 780 us
  waiting for transfers between devices  273 us (35%)
  blocking collectives  183 us (23%)
  matrix products  140 us (18%)
  local copies, waits for them, and re-layouts  117 us (15%)
  other arithmetic  46.3 us (6%)
  starting transfers between devices  18.8 us (2%)
    all_to_all x1, waiting for transfers between devices, local(): lax.all_to_all(depthwise, 'col', split_axis=2, concat_axis=3, tiled=True)  237 us
    all_to_all x1, blocking collectives, local(): lax.all_to_all(forced, 'row', split_axis=1, concat_axis=3, tiled=True)  143 us
    dot_general x1, matrix products, local(): jnp.einsum('xczy,ypk->pcxzk', lax.all_to_all(depthwise, 'col', split_axis...  90.5 us
    dot_general x1, matrix products, local(): jnp.einsum('cxyz,zw->xcwy', lax.all_to_all(forced, 'row', split_axis=1, c...  45.8 us
    all_to_all x1, blocking collectives, local(): lax.all_to_all(outgoing.reshape(columns, CAP, 3, TY, depth), 'col', split...  40.7 us
    all_to_all x1, waiting for transfers between devices, local(): lax.all_to_all(outgoing_tiles, 'col', split_axis=0, concat_axis=0, tiled=...  36.5 us
    mul x1, other arithmetic, local(): jnp.cos(phase) * damping[None, :]  35.3 us
    all_to_all x2, local copies, waits for them, and re-layouts, local(): lax.all_to_all(depthwise, 'col', split_axis=2, concat_axis=3, tiled=True)  30.2 us
  transfers between devices with their start and end apart: 3, of which 2 were waited for; matrix products, arithmetic and copies ran while one was open for 6% of the time, Pallas kernels for 0%

commit v1 on v0

v1 whole, which is shorter than its diff:
```python
import jax
import jax.numpy as jnp
from jax import lax
from jax.experimental import pallas as pl
from jax.experimental.pallas import tpu as pltpu
from jax.sharding import PartitionSpec as P


TY = 8
K = 4
CAP = 8

smoothing = 1.0


f32 = jnp.float32
bf16 = jnp.bfloat16
ANY = pl.BlockSpec(memory_space=pl.ANY)
SMEM = pl.BlockSpec(memory_space=pltpu.SMEM)
VMEM = pl.BlockSpec(memory_space=pltpu.VMEM)
NT = (((1,), (1,)), ((), ()))
NN = (((1,), (0,)), ((), ()))


def split(x):
    hi = x.astype(bf16)
    return hi, (x - hi.astype(f32)).astype(bf16)


def dot3(a, b, dims):
    dot = lambda p, q: lax.dot_general(p, q, dims, preferred_element_type=f32)
    return dot(a[0], b[0]) + (dot(a[0], b[1]) + dot(a[1], b[0]))


def swap(x, axis, m, n):
    return lax.ppermute(x, axis, [(i, i ^ m) for i in range(n)])


def gather_tiles(meta, served, velocity, columns, per_row):
    comps, _, _, depth = velocity.shape

    def body(meta_ref, served_ref, vel, *rest):
        outs = rest[:columns]
        pool, sem_in, sem_out = rest[columns:]
        mine = meta_ref[1]
        order = list(range(columns))[::-1]
        loads = {}
        for m in order:
            for s in range(CAP):
                t = served_ref[mine ^ m, s]
                band = pl.multiple_of((t % per_row) * TY, TY)
                loads[m, s] = pltpu.make_async_copy(
                    vel.at[:, t // per_row, pl.ds(band, TY), :], pool.at[m, s], sem_in.at[m, s]
                )
                loads[m, s].start()
        stores = []
        for m in order:
            for s in range(CAP):
                loads[m, s].wait()
            stores.append(pltpu.make_async_copy(pool.at[m], outs[m], sem_out.at[m]))
            stores[-1].start()
        for cp in stores:
            cp.wait()

    return pl.pallas_call(
        body,
        in_specs=[SMEM, SMEM, ANY],
        out_specs=[ANY] * columns,
        out_shape=[jax.ShapeDtypeStruct((CAP, comps, TY, depth), f32)] * columns,
        scratch_shapes=[
            pltpu.VMEM((columns, CAP, comps, TY, depth), f32),
            pltpu.SemaphoreType.DMA((columns, CAP)),
            pltpu.SemaphoreType.DMA((columns,)),
        ],
        name="gather_tiles",
    )(meta, served, velocity)


def markers(slot, fetched, amplitude, lateral, vertical, wall, surface):
    columns = len(fetched)
    blocks, _, count = amplitude.shape
    _, comps, _, depth = fetched[0].shape
    rows = comps * TY

    def body(slot_ref, *refs):
        ins = refs[:columns]
        amp, lat, ver, wal, sur = refs[columns : columns + 5]
        outs = refs[columns + 5 : 2 * columns + 5]
        force = refs[2 * columns + 5]
        tin, tout, sem_in, sem_out = refs[2 * columns + 6 :]
        loads = [
            pltpu.make_async_copy(ins[m], tin.at[pl.ds(m * CAP, CAP)], sem_in.at[m])
            for m in range(columns)
        ]
        for cp in loads:
            cp.start()
        tout[...] = jnp.zeros(tout.shape, f32)
        for cp in loads:
            cp.wait()
        for b in range(blocks):
            v = split(ver[b])
            weight = [amp[b, k : k + 1, :] * lat[b] for k in range(K)]
            picked = jnp.concatenate(
                [tin[slot_ref[b * K + k]].reshape(rows, depth) for k in range(K)], axis=0
            )
            inner = dot3(split(picked), v, NN)
            shares = [[None] * comps for _ in range(K)]
            for c in range(comps):
                total = jnp.zeros((TY, count), f32)
                for k in range(K):
                    at = k * rows + c * TY
                    total = total + weight[k] * inner[at : at + TY]
                mf = wal[b, c : c + 1, :] - jnp.sum(total, axis=0, keepdims=True)
                force[b, c : c + 1, :] = mf
                scaled = sur[b : b + 1, :] * mf
                for k in range(K):
                    shares[k][c] = weight[k] * scaled
            share = jnp.concatenate([shares[k][c] for k in range(K) for c in range(comps)], axis=0)
            spread = dot3(split(share), v, NT)
            for k in range(K):
                tout[slot_ref[b * K + k]] = spread[k * rows : (k + 1) * rows].reshape(
                    comps, TY, depth
                )
        stores = [
            pltpu.make_async_copy(tout.at[pl.ds(m * CAP, CAP)], outs[m], sem_out.at[m])
            for m in range(columns)
        ]
        for cp in stores[::-1]:
            cp.start()
        for cp in stores:
            cp.wait()

    tile = (CAP, comps, TY, depth)
    pool = pltpu.VMEM((columns * CAP, comps, TY, depth), f32)
    out = pl.pallas_call(
        body,
        in_specs=[SMEM] + [ANY] * columns + [VMEM] * 5,
        out_specs=[ANY] * columns + [VMEM],
        out_shape=[jax.ShapeDtypeStruct(tile, f32)] * columns
        + [jax.ShapeDtypeStruct(wall.shape, f32)],
        scratch_shapes=[
            pool,
            pool,
            pltpu.SemaphoreType.DMA((columns,)),
            pltpu.SemaphoreType.DMA((columns,)),
        ],
        name="markers",
    )(slot, *fetched, amplitude, lateral, vertical, wall, surface)
    return out[:columns], out[columns]


def fill(meta, served, incoming, velocity, chunk, rows_n, per_row, after):
    columns = len(incoming)
    _, width_x, height, depth = velocity.shape
    xl, c0, nc = chunk
    planes = width_x // rows_n
    extra = len(after)

    def body(meta_ref, served_ref, *refs):
        ins = refs[:columns]
        vel = refs[columns]
        rest = refs[columns + 1 + extra :]
        outs = rest[:rows_n]
        buf, inc, sem_in, sem_v, sem_out = rest[rows_n:]
        me, mine = meta_ref[0], meta_ref[1]
        loads = []
        for m in range(rows_n):
            cp = pltpu.make_async_copy(
                vel.at[pl.ds(c0, nc), (me ^ m) * planes + xl], buf.at[m], sem_v.at[m]
            )
            cp.start()
            loads.append(cp)
        for m in range(columns):
            cp = pltpu.make_async_copy(
                ins[m].at[:, pl.ds(c0, nc)], inc.at[pl.ds(m * CAP, CAP)], sem_in.at[m]
            )
            cp.start()
            loads.append(cp)
        for cp in loads:
            cp.wait()

        def add(s, carry):
            t = served_ref[mine ^ (s // CAP), s % CAP]
            plane = t // per_row
            band = pl.multiple_of((t % per_row) * TY, TY)

            @pl.when(plane % planes == xl)
            def _():
                to = (plane // planes) ^ me
                buf[to, :, pl.ds(band, TY), :] += inc[s]

            return carry

        lax.fori_loop(0, columns * CAP, add, 0)
        stores = [pltpu.make_async_copy(buf.at[m], outs[m], sem_out.at[m]) for m in range(rows_n)]
        for cp in stores[::-1]:
            cp.start()
        for cp in stores:
            cp.wait()

    return pl.pallas_call(
        body,
        in_specs=[SMEM, SMEM] + [ANY] * (columns + 1 + extra),
        out_specs=[ANY] * rows_n,
        out_shape=[jax.ShapeDtypeStruct((nc, height, depth), f32)] * rows_n,
        scratch_shapes=[
            pltpu.VMEM((rows_n, nc, height, depth), f32),
            pltpu.VMEM((columns * CAP, nc, TY, depth), f32),
            pltpu.SemaphoreType.DMA((columns,)),
            pltpu.SemaphoreType.DMA((rows_n,)),
            pltpu.SemaphoreType.DMA((rows_n,)),
        ],
        name="fill",
    )(meta, served, *incoming, velocity, *after)


def axial_weights(meta, z_inverse, rows_n, columns, after):
    total = z_inverse.shape[0]
    depth, width = total // rows_n, total // columns
    extra = len(after)

    def body(meta_ref, z, *rest):
        hi, lo = rest[extra:]
        a, b = split(z[...].T)
        hi[...] = a
        lo[...] = b

    grid_spec = pltpu.PrefetchScalarGridSpec(
        num_scalar_prefetch=1,
        grid=(columns // 2, rows_n),
        in_specs=[
            pl.BlockSpec((depth, 2 * width), lambda o, i, s: (s[0] ^ i, (s[1] // 2) ^ o))
        ]
        + [ANY] * extra,
        out_specs=[pl.BlockSpec((2 * width, depth), lambda o, i, s: (o, i))] * 2,
    )
    return pl.pallas_call(
        body,
        grid_spec=grid_spec,
        out_shape=[jax.ShapeDtypeStruct((total, total), bf16)] * 2,
        name="axial_weights",
    )(meta, z_inverse, *after)


def solve(meta, planes, weights, after):
    rows_n = len(planes)
    extra = len(after)
    nc, height, depth = planes[0].shape
    total = weights[0].shape[0]
    columns = meta[1]
    width = total // columns

    def body(meta_ref, *refs):
        ins = refs[:rows_n]
        hi, lo = refs[rows_n : rows_n + 2]
        outs = refs[rows_n + 2 + extra : rows_n + 2 + extra + columns]
        fh, fl = refs[rows_n + 2 + extra + columns :]
        for m in range(rows_n):
            a, b = split(ins[m][0])
            fh[:, m * depth : (m + 1) * depth] = a
            fl[:, m * depth : (m + 1) * depth] = b
        field = (fh[...], fl[...])
        odd = meta_ref[1] % 2
        for o in range(columns // 2):
            got = dot3(
                (hi[o * 2 * width : (o + 1) * 2 * width], lo[o * 2 * width : (o + 1) * 2 * width]),
                field,
                NT,
            )
            first, second = got[:width], got[width:]
            outs[2 * o][0] = jnp.where(odd == 0, first, second)
            outs[2 * o + 1][0] = jnp.where(odd == 0, second, first)

    return pl.pallas_call(
        body,
        grid=(nc,),
        in_specs=[SMEM]
        + [pl.BlockSpec((1, height, depth), lambda u: (u, 0, 0))] * rows_n
        + [pl.BlockSpec((total, total), lambda u: (0, 0))] * 2
        + [ANY] * extra,
        out_specs=[pl.BlockSpec((1, width, height), lambda u: (u, 0, 0))] * columns,
        out_shape=[jax.ShapeDtypeStruct((nc, width, height), f32)] * columns,
        scratch_shapes=[pltpu.VMEM((height, total), bf16)] * 2,
        name="solve",
    )(meta[0], *planes, *weights, *after)


def fourier_table(ny, blocks, after):
    half = ny // 2
    height = half // blocks
    wavenumber = jnp.arange(half, dtype=jnp.int32)

    def waves(places):
        phase = (places[:, None] * wavenumber[None, :] % ny).astype(f32) * (2.0 * jnp.pi / ny)
        return jnp.cos(phase), jnp.sin(phase)

    wave = wavenumber.astype(f32)
    damping = 1.0 / (1.0 + 4.0 * smoothing * jnp.sin(jnp.pi * wave / ny) ** 2) / jnp.sqrt(f32(ny))
    coarse = waves(jnp.arange(blocks, dtype=jnp.int32) * height)
    fine = waves(jnp.arange(height, dtype=jnp.int32))
    fine = (fine[0] * damping[None, :], fine[1] * damping[None, :])
    middle = jnp.where(wavenumber % 2 == 0, damping, -damping)[None, :]
    block = min(half, 512)
    per = half // block
    extra = len(after)

    def body(cc, cs, fc, fs, *rest):
        hi, lo = rest[extra:]
        p = pl.program_id(1)
        a, b = cc[0], cs[0]

        @pl.when(p == 0)
        def _():
            hi[...], lo[...] = split(a * fc[...] - b * fs[...])

        @pl.when(p == 1)
        def _():
            hi[...], lo[...] = split(-(b * fc[...] + a * fs[...]))

    coarse_spec = pl.BlockSpec((1, 1, block), lambda n, p, m: (m, 0, n))
    fine_spec = pl.BlockSpec((height, block), lambda n, p, m: (0, n))
    hi, lo = pl.pallas_call(
        body,
        grid=(per, 2, blocks),
        in_specs=[coarse_spec, coarse_spec, fine_spec, fine_spec] + [ANY] * extra,
        out_specs=[pl.BlockSpec((height, block), lambda n, p, m: (m, p * per + n))] * 2,
        out_shape=[jax.ShapeDtypeStruct((half, ny), bf16)] * 2,
        name="fourier_table",
    )(coarse[0][:, None, :], coarse[1][:, None, :], *fine, *after)
    return hi, lo, middle


def transform(meta, pieces, table, chunk, shape, spectrum, after):
    columns = len(pieces)
    nc, width, height = pieces[0].shape
    ny = height * columns
    half = ny // 2
    low = columns // 2
    rows = nc * width
    xl, c0, _ = chunk
    block = min(half, 256)
    per = half // block
    carried = [] if spectrum is None else [spectrum]
    extra = len(after) + len(carried)

    def body(meta_ref, *refs):
        ins = refs[:columns]
        hi, lo, mid = refs[columns : columns + 3]
        out, held, eh, el, oh, ol, alone = refs[columns + 3 + extra :]
        mine = meta_ref[1]
        n = pl.program_id(0)

        @pl.when(n == 0)
        def _():
            for m in range(columns):
                held[mine ^ m] = ins[m][...].reshape(rows, height)
            lane = lax.broadcasted_iota(jnp.int32, (height, height), 1)
            sub = lax.broadcasted_iota(jnp.int32, (height, height), 0)
            turn = jnp.where(lane + sub == height, 1.0, 0.0).astype(bf16)
            first = lax.broadcasted_iota(jnp.int32, (rows, height), 1) == 0
            for q in range(low):
                a, b = split(held[columns - 1 - q])
                dot = lambda x: lax.dot_general(x, turn, NN, preferred_element_type=f32)
                back = dot(a) + dot(b)
                edge = held[columns - q] if q > 0 else jnp.zeros((rows, height), f32)
                back = jnp.where(first, edge, back)
                here = held[q]
                at = slice(q * height, (q + 1) * height)
                eh[:, at], el[:, at] = split(here + back)
                oh[:, at], ol[:, at] = split(here - back)
            alone[...] = jnp.broadcast_to(held[low][:, 0:1], alone.shape)

        @pl.when(n < per)
        def _():
            got = dot3((eh[...], el[...]), (hi[...], lo[...]), NN)
            got = got + alone[:, 0:1] * mid[...]
            out[...] = got.reshape(1, nc, 1, width, block)

        @pl.when(n >= per)
        def _():
            got = dot3((oh[...], ol[...]), (hi[...], lo[...]), NN)
            out[...] = got.reshape(1, nc, 1, width, block)

    return pl.pallas_call(
        body,
        grid=(2 * per,),
        in_specs=[SMEM]
        + [pl.BlockSpec((nc, width, height), lambda n: (0, 0, 0))] * columns
        + [pl.BlockSpec((half, block), lambda n: (0, n))] * 2
        + [pl.BlockSpec((1, block), lambda n: (0, n % per))]
        + [ANY] * extra,
        out_specs=pl.BlockSpec(
            (1, nc, 1, width, block), lambda n: (n // per, c0 // nc, xl, 0, n % per)
        ),
        out_shape=jax.ShapeDtypeStruct(shape, f32),
        scratch_shapes=[pltpu.VMEM((columns, rows, height), f32)]
        + [pltpu.VMEM((rows, half), bf16)] * 4
        + [pltpu.VMEM((rows, 128), f32)],
        input_output_aliases={columns + 4: 0} if carried else {},
        name="transform",
    )(meta, *pieces, *table, *carried, *after)


def chunks_of(comps, planes):
    last = planes - 1
    parts = [(0, comps - 1, 1), (0, 0, comps - 1)]
    parts += [(x, 0, comps) for x in range(1, last)]
    parts += [(last, 0, comps - 1), (last, comps - 1, 1)]
    return parts


def local(velocity, z_inverse, tiles, amplitude, lateral, vertical, wall_velocity, surface):
    comps, width_x, height, depth = velocity.shape
    columns = lax.axis_size("col")
    rows_n = lax.axis_size("row")
    me = lax.axis_index("row").astype(jnp.int32)
    mine = lax.axis_index("col").astype(jnp.int32)
    meta = jnp.stack([me, mine])
    per_row = height // TY
    tile_count = width_x * per_row
    requests = tiles.reshape(-1)
    count = requests.shape[0]
    holder = requests // tile_count
    within = requests % tile_count
    order = jnp.arange(count, dtype=jnp.int32)
    place = jnp.sum(
        ((holder[:, None] == holder[None, :]) & (order[None, :] < order[:, None])).astype(
            jnp.int32
        ),
        axis=1,
    )
    lanes = 128
    who = jnp.arange(columns, dtype=jnp.int32)[:, None, None]
    spot = jnp.arange(lanes, dtype=jnp.int32)[None, :, None]
    hit = (holder[None, None, :] == who) & (place[None, None, :] == spot)
    wanted = jnp.sum(jnp.where(hit, within[None, None, :], 0), axis=2)
    slot = (holder ^ mine) * CAP + place
    served = lax.all_to_all(wanted, "col", split_axis=0, concat_axis=0, tiled=True)
    asked = gather_tiles(meta, served, velocity, columns, per_row)
    fetched = [asked[0]] + [None] * (columns - 1)
    for m in reversed(range(1, columns)):
        fetched[m] = swap(asked[m], "col", m, columns)
    weights = axial_weights(meta, z_inverse, rows_n, columns, [asked[0]])
    outgoing, marker_force = markers(
        slot, fetched, amplitude, lateral, vertical, wall_velocity, surface
    )
    incoming = [outgoing[0]] + [None] * (columns - 1)
    for m in reversed(range(1, columns)):
        incoming[m] = swap(outgoing[m], "col", m, columns)
    table = fourier_table(height * columns, max(columns // 2, 1), [outgoing[0]])
    planes = width_x // rows_n
    chunks = chunks_of(comps, planes)
    solved = []
    sent = [None] * len(chunks)
    got = [None] * len(chunks)

    def send(j, after):
        sent[j] = fill(meta, served, incoming, velocity, chunks[j], rows_n, per_row, after)
        got[j] = [sent[j][0]] + [None] * (rows_n - 1)
        for m in reversed(range(1, rows_n)):
            got[j][m] = swap(sent[j][m], "row", m, rows_n)

    send(0, [weights[0], table[0]])
    send(1, [sent[0][0]])
    for j in range(len(chunks)):
        ahead = [sent[j + 1][0]] if j + 1 < len(chunks) else []
        out = solve((meta, columns), got[j], weights, ahead)
        pieces = [out[0]] + [None] * (columns - 1)
        for m in reversed(range(1, columns)):
            pieces[m] = swap(out[m], "col", m, columns)
        solved.append(pieces)
        if j + 2 < len(chunks):
            send(j + 2, [out[0]])
    last = [solved[-1][0]]
    total = depth * rows_n
    shape = (2, comps, planes, total // columns, height * columns // 2)
    spectrum = None
    for j in range(len(chunks)):
        spectrum = transform(
            meta, solved[j], table, chunks[j], shape, spectrum, last if j == 0 else []
        )
    return (spectrum, marker_force)


def solution(mesh):
    in_specs = (
        P(None, None, "col", "row"),
        P(),
        P(("row", "col"), None),
        P(("row", "col"), None, None),
        P(("row", "col"), None, None),
        P(("row", "col"), None, None),
        P(("row", "col"), None, None),
        P(("row", "col"), None),
    )
    out_specs = (P(None, None, "row", "col", None), P(("row", "col"), None, None))

    return jax.shard_map(local, mesh=mesh, in_specs=in_specs, out_specs=out_specs, check_vma=False)
```

time: 788 us -> 570 us (0.72)
  the two profiles are of different devices: /device:TPU:0 before, /device:TPU:8 now
where the time goes in v1:
time: 570 us; the launch traced here: 568 us
  waiting for transfers between devices  262 us (46%)
  Pallas kernels  181 us (32%)
  starting transfers between devices  103 us (18%)
  local copies, waits for them, and re-layouts  11.5 us (2%)
  other arithmetic  9.14 us (2%)
    ppermute x74, waiting for transfers between devices, swap(): return lax.ppermute(x, axis, [(i, i ^ m) for i in range(n)])  259 us
    ppermute x74, starting transfers between devices, swap(): return lax.ppermute(x, axis, [(i, i ^ m) for i in range(n)])  96.8 us
    pallas_call x6, Pallas kernels, transform(): pl.pallas_call(body, grid=(2 * per,), in_specs=[SMEM] + [pl.BlockSpec((nc...  65.4 us
    pallas_call x6, Pallas kernels, solve(): pl.pallas_call(body, grid=(nc,), in_specs=[SMEM] + [pl.BlockSpec((1, heig...  43.3 us
    pallas_call x6, Pallas kernels, fill(): pl.pallas_call(body, in_specs=[SMEM, SMEM] + [ANY] * (columns + 1 + extra...  37.8 us
    pallas_call x1, Pallas kernels, axial_weights(): pl.pallas_call(body, grid_spec=grid_spec, out_shape=[jax.ShapeDtypeStruct...  11.6 us
    unnamed x133, local copies, waits for them, and re-layouts  11.5 us
  transfers between devices with their start and end apart: 75, of which 36 were waited for; matrix products, arithmetic and copies ran while one was open for 2% of the time, Pallas kernels for 27%

profile of v1, /device:TPU:8, one launch (start us, length us, event | category | flops | bytes accessed | tf_op | source)
XLA Modules:
  0.0 567.9 jit_solution(5354638640145498311)
XLA Ops:
  36.0 16.1 %collective-permute-done.3.refs_4_ = f32[8,3,8,256]{3,2,1,0:T(8,128)S(1)} collective-permute-done((f32[8,3,8,256]{3,2,1,0:T(8,128)}, f32[8,3,8,256]{3,2,1,0:T(8,128)S(1)}, u32[]{:S(2)}, u32[]{:S(2)}) %collective-permute-start.3) | collective-permute-done | bytes 196640 | tf_op jit(solution)/shard_map/ppermute | solution.py:36
  86.3 11.6 %axial_weights.1 = (bf16[1024,1024]{1,0:T(8,128)(2,1)}, bf16[1024,1024]{1,0:T(8,128)(2,1)}) custom-call(s32[2]{0:T(128)} %pad_add_fusion.meta_ref, f32[1024,1024]{1,0:T(8,128)} %z.1, f32[8,3,8,256]{3,2,1,0:T(8,128)} %get-tuple-element.95.refs_0_.rest_0_), custom_call_target="tpu_custom_call" | custom-call | tf_op jit(solution)/shard_map/axial_weights/pallas_call | solution.py:237
  97.9 11.0 %fourier_table.1 = (bf16[1024,2048]{1,0:T(8,128)(2,1)}, bf16[1024,2048]{1,0:T(8,128)(2,1)}) custom-call(f32[4,1,1024]{2,1,0:T(1,128)} %get-tuple-element.199.cc, f32[4,1,1024]{2,1,0:T(1,128)} %get-tuple-element.198.cs, f32[256,1024]{1,0:T(8,128)} %get-tuple-element.201.fc, f32[256,1024]{1,0:T(8,128)} %get-tuple-element.200.fs, ...), custom_call_target="tpu_custom_call" | custom-call | tf_op jit(solution)/shard_map/fourier_table/pallas_call | solution.py:322
  128.2 28.3 %collective-permute-done.18.refs_2_ = f32[1,256,256]{2,1,0:T(8,128)S(1)} collective-permute-done((f32[1,256,256]{2,1,0:T(8,128)S(1)}, f32[1,256,256]{2,1,0:T(8,128)S(1)}, u32[]{:S(2)}, u32[]{:S(2)}) %collective-permute-start.18) | collective-permute-done | bytes 262176 | tf_op jit(solution)/shard_map/ppermute | solution.py:36
  179.3 7.2 %solve.7 = (f32[2,128,256]{2,1,0:T(8,128)}, f32[2,128,256]{2,1,0:T(8,128)}, f32[2,128,256]{2,1,0:T(8,128)}, f32[2,128,256]{2,1,0:T(8,128)}, f32[2,128,256]{2,1,0...) custom-call(s32[2]{0:T(128)} %pad_add_fusion.meta_ref, ...), custom_call_target="tpu_custom_call" | custom-call | tf_op jit(solution)/shard_map/solve/pallas_call | solution.py:274
  192.1 9.4 %collective-permute-done.71.refs_5_ = f32[1,128,256]{2,1,0:T(8,128)S(1)} collective-permute-done((f32[1,128,256]{2,1,0:T(8,128)S(1)}, f32[1,128,256]{2,1,0:T(8,128)S(1)}, u32[]{:S(2)}, u32[]{:S(2)}) %collective-permute-start.71) | collective-permute-done | bytes 131104 | tf_op jit(solution)/shard_map/ppermute | solution.py:36
  242.8 9.3 %solve.8 = (f32[3,128,256]{2,1,0:T(8,128)}, f32[3,128,256]{2,1,0:T(8,128)}, f32[3,128,256]{2,1,0:T(8,128)}, f32[3,128,256]{2,1,0:T(8,128)}, f32[3,128,256]{2,1,0...) custom-call(s32[2]{0:T(128)} %pad_add_fusion.meta_ref, ...), custom_call_target="tpu_custom_call" | custom-call | tf_op jit(solution)/shard_map/solve/pallas_call | solution.py:274
  274.7 12.9 %collective-permute-done.54.refs_2_ = f32[3,128,256]{2,1,0:T(8,128)S(1)} collective-permute-done((f32[3,128,256]{2,1,0:T(8,128)}, f32[3,128,256]{2,1,0:T(8,128)S(1)}, u32[]{:S(2)}, u32[]{:S(2)}) %collective-permute-start.54) | collective-permute-done | bytes 393248 | tf_op jit(solution)/shard_map/ppermute | solution.py:36
  295.0 9.1 %solve.9 = (f32[3,128,256]{2,1,0:T(8,128)}, f32[3,128,256]{2,1,0:T(8,128)}, f32[3,128,256]{2,1,0:T(8,128)}, f32[3,128,256]{2,1,0:T(8,128)}, f32[3,128,256]{2,1,0...) custom-call(s32[2]{0:T(128)} %pad_add_fusion.meta_ref, ...), custom_call_target="tpu_custom_call" | custom-call | tf_op jit(solution)/shard_map/solve/pallas_call | solution.py:274
  318.9 7.8 %collective-permute-done.58.refs_6_ = f32[3,128,256]{2,1,0:T(8,128)S(1)} collective-permute-done((f32[3,128,256]{2,1,0:T(8,128)}, f32[3,128,256]{2,1,0:T(8,128)S(1)}, u32[]{:S(2)}, u32[]{:S(2)}) %collective-permute-start.58) | collective-permute-done | bytes 393248 | tf_op jit(solution)/shard_map/ppermute | solution.py:36
  337.3 12.3 %collective-permute-done.27.refs_2_ = f32[1,256,256]{2,1,0:T(8,128)S(1)} collective-permute-done((f32[1,256,256]{2,1,0:T(8,128)}, f32[1,256,256]{2,1,0:T(8,128)S(1)}, u32[]{:S(2)}, u32[]{:S(2)}) %collective-permute-start.27) | collective-permute-done | bytes 262176 | tf_op jit(solution)/shard_map/ppermute | solution.py:36
  366.4 10.9 %collective-permute-done.29.refs_1_ = f32[1,128,256]{2,1,0:T(8,128)S(1)} collective-permute-done((f32[1,128,256]{2,1,0:T(8,128)}, f32[1,128,256]{2,1,0:T(8,128)S(1)}, u32[]{:S(2)}, u32[]{:S(2)}) %collective-permute-start.29) | collective-permute-done | bytes 131104 | tf_op jit(solution)/shard_map/ppermute | solution.py:36
  377.3 10.2 %collective-permute-done.30.refs_2_ = f32[1,128,256]{2,1,0:T(8,128)S(1)} collective-permute-done((f32[1,128,256]{2,1,0:T(8,128)}, f32[1,128,256]{2,1,0:T(8,128)S(1)}, u32[]{:S(2)}, u32[]{:S(2)}) %collective-permute-start.30) | collective-permute-done | bytes 131104 | tf_op jit(solution)/shard_map/ppermute | solution.py:36
  392.5 7.2 %solve.11 = (f32[2,128,256]{2,1,0:T(8,128)}, f32[2,128,256]{2,1,0:T(8,128)}, f32[2,128,256]{2,1,0:T(8,128)}, f32[2,128,256]{2,1,0:T(8,128)}, f32[2,128,256]{2,1,...) custom-call(s32[2]{0:T(128)} %pad_add_fusion.meta_ref, ...), custom_call_target="tpu_custom_call" | custom-call | tf_op jit(solution)/shard_map/solve/pallas_call | solution.py:274
  403.2 20.5 %collective-permute-done.50.refs_5_ = f32[3,128,256]{2,1,0:T(8,128)} collective-permute-done((f32[3,128,256]{2,1,0:T(8,128)}, f32[3,128,256]{2,1,0:T(8,128)}, u32[]{:S(2)}, u32[]{:S(2)}) %collective-permute-start.50) | collective-permute-done | bytes 393248 | tf_op jit(solution)/shard_map/ppermute | solution.py:36
  433.4 14.7 %collective-permute-done.52.refs_7_ = f32[3,128,256]{2,1,0:T(8,128)} collective-permute-done((f32[3,128,256]{2,1,0:T(8,128)}, f32[3,128,256]{2,1,0:T(8,128)}, u32[]{:S(2)}, u32[]{:S(2)}) %collective-permute-start.52) | collective-permute-done | bytes 393248 | tf_op jit(solution)/shard_map/ppermute | solution.py:36
  455.8 12.5 %collective-permute-done.42.refs_4_ = f32[2,128,256]{2,1,0:T(8,128)S(1)} collective-permute-done((f32[2,128,256]{2,1,0:T(8,128)}, f32[2,128,256]{2,1,0:T(8,128)S(1)}, u32[]{:S(2)}, u32[]{:S(2)}) %collective-permute-start.42) | collective-permute-done | bytes 262176 | tf_op jit(solution)/shard_map/ppermute | solution.py:36
  481.3 11.4 %collective-permute-done.44.refs_6_ = f32[2,128,256]{2,1,0:T(8,128)S(1)} collective-permute-done((f32[2,128,256]{2,1,0:T(8,128)}, f32[2,128,256]{2,1,0:T(8,128)S(1)}, u32[]{:S(2)}, u32[]{:S(2)}) %collective-permute-start.44) | collective-permute-done | bytes 262176 | tf_op jit(solution)/shard_map/ppermute | solution.py:36
  502.3 9.1 %transform.6.refs_11_ = f32[2,3,4,128,1024]{4,3,2,1,0:T(8,128)} custom-call(s32[2]{0:T(128)} %pad_add_fusion.meta_ref, f32[1,128,256]{2,1,0:T(8,128)} %get-tuple-element.122.refs_9_.refs_0_, f32[1,128,256]{2,1,0:T(8,128)} %copy-done.50, f32[1,128,256]{2,1,0:T(8,128)} %copy-done.51, f32[1,128,256]{2,1,0:T(8,128)} %copy-done.52, f32[1,128,256]{2,1,0:T(8,128)} %copy-done.53, ...), custom_call_target="tpu_custom_call" | custom-call | tf_op jit(solution)/shard_map/transform/pallas_call | solution.py:384
  511.4 10.8 %transform.7.refs_11_ = f32[2,3,4,128,1024]{4,3,2,1,0:T(8,128)} custom-call(s32[2]{0:T(128)} %pad_add_fusion.meta_ref, f32[2,128,256]{2,1,0:T(8,128)} %get-tuple-element.124.refs_9_.refs_0_, f32[2,128,256]{2,1,0:T(8,128)} %copy-done.27, f32[2,128,256]{2,1,0:T(8,128)} %collective-permute-done.61.refs_2_, ...), custom_call_target="tpu_custom_call", output_to_operand_aliasing={{}: (12, {})} | custom-call | tf_op jit(solution)/shard_map/transform/pallas_call | solution.py:384
  522.2 13.0 %transform.8.refs_11_ = f32[2,3,4,128,1024]{4,3,2,1,0:T(8,128)} custom-call(s32[2]{0:T(128)} %pad_add_fusion.meta_ref, f32[3,128,256]{2,1,0:T(8,128)} %get-tuple-element.132.refs_9_.refs_0_, f32[3,128,256]{2,1,0:T(8,128)} %copy-done.17, f32[3,128,256]{2,1,0:T(8,128)} %copy-done.18, f32[3,128,256]{2,1,0:T(8,128)} %copy-done.19, ...), custom_call_target="tpu_custom_call", output_to_operand_aliasing={{}: (12, {})} | custom-call | tf_op jit(solution)/shard_map/transform/pallas_call | solution.py:384
  535.2 12.7 %transform.9.refs_11_ = f32[2,3,4,128,1024]{4,3,2,1,0:T(8,128)} custom-call(s32[2]{0:T(128)} %pad_add_fusion.meta_ref, f32[3,128,256]{2,1,0:T(8,128)} %get-tuple-element.134.refs_9_.refs_0_, f32[3,128,256]{2,1,0:T(8,128)} %copy-done.23, f32[3,128,256]{2,1,0:T(8,128)} %copy-done.24, f32[3,128,256]{2,1,0:T(8,128)} %copy-done.25, ...), custom_call_target="tpu_custom_call", output_to_operand_aliasing={{}: (12, {})} | custom-call | tf_op jit(solution)/shard_map/transform/pallas_call | solution.py:384
  547.9 10.8 %transform.10.refs_11_ = f32[2,3,4,128,1024]{4,3,2,1,0:T(8,128)} custom-call(s32[2]{0:T(128)} %pad_add_fusion.meta_ref, f32[2,128,256]{2,1,0:T(8,128)} %get-tuple-element.151.refs_0_, f32[2,128,256]{2,1,0:T(8,128)} %copy-done.30, f32[2,128,256]{2,1,0:T(8,128)} %copy-done.31, f32[2,128,256]{2,1,0:T(8,128)} %copy-done.32, ...), custom_call_target="tpu_custom_call", output_to_operand_aliasing={{}: (12, {})} | custom-call | tf_op jit(solution)/shard_map/transform/pallas_call | solution.py:384
  558.7 9.1 %transform.11 = f32[2,3,4,128,1024]{4,3,2,1,0:T(8,128)} custom-call(s32[2]{0:T(128)} %pad_add_fusion.meta_ref, f32[1,128,256]{2,1,0:T(8,128)} %get-tuple-element.139.refs_11_.refs_0_, f32[1,128,256]{2,1,0:T(8,128)} %copy-done.57, f32[1,128,256]{2,1,0:T(8,128)} %copy-done.58, ...), custom_call_target="tpu_custom_call", output_to_operand_aliasing={{}: (12, {})} | custom-call | tf_op jit(solution)/shard_map/transform/pallas_call | solution.py:384
  (295 shorter events, 278.7 us)
Async XLA Ops:
  124.2 45.0 %collective-permute-start.14 = (f32[2,256,256]{2,1,0:T(8,128)}, f32[2,256,256]{2,1,0:T(8,128)S(1)}, u32[]{:S(2)}, u32[]{:S(2)}) collective-permute-start(f32[2,256,256]{2,1,0:T(8,128)} %get-tuple-element.115), channel_id=1, source_target_pairs={{0,8},{8,0},{16,24},{24,16},{1,9},{9,1},{17,25},{25,17},{2,10},{10... | collective-permute-start | bytes 1572872 | tf_op jit(solution)/shard_map/ppermute | solution.py:36
  124.6 52.4 %collective-permute-start.15 = (f32[2,256,256]{2,1,0:T(8,128)}, f32[2,256,256]{2,1,0:T(8,128)S(1)}, u32[]{:S(2)}, u32[]{:S(2)}) collective-permute-start(f32[2,256,256]{2,1,0:T(8,128)} %get-tuple-element.116), channel_id=1, source_target_pairs={{0,16},{8,24},{16,0},{24,8},{1,17},{9,25},{17,1},{25,9},{2,18},{10... | collective-permute-start | bytes 1572872 | tf_op jit(solution)/shard_map/ppermute | solution.py:36
  124.6 53.8 %collective-permute-start.16 = (f32[2,256,256]{2,1,0:T(8,128)}, f32[2,256,256]{2,1,0:T(8,128)S(1)}, u32[]{:S(2)}, u32[]{:S(2)}) collective-permute-start(f32[2,256,256]{2,1,0:T(8,128)} %get-tuple-element.117), channel_id=1, source_target_pairs={{0,24},{8,16},{16,8},{24,0},{1,25},{9,17},{17,9},{25,1},{2,26},{10... | collective-permute-start | bytes 1572872 | tf_op jit(solution)/shard_map/ppermute | solution.py:36
  190.4 45.6 %collective-permute-start.23 = (f32[3,256,256]{2,1,0:T(8,128)}, f32[3,256,256]{2,1,0:T(8,128)S(1)}, u32[]{:S(2)}, u32[]{:S(2)}) collective-permute-start(f32[3,256,256]{2,1,0:T(8,128)} %get-tuple-element.129), channel_id=1, source_target_pairs={{0,8},{8,0},{16,24},{24,16},{1,9},{9,1},{17,25},{25,17},{2,10},{10... | collective-permute-start | bytes 2359304 | tf_op jit(solution)/shard_map/ppermute | solution.py:36
  262.8 46.7 %collective-permute-start.55 = (f32[3,128,256]{2,1,0:T(8,128)}, f32[3,128,256]{2,1,0:T(8,128)S(1)}, u32[]{:S(2)}, u32[]{:S(2)}) collective-permute-start(f32[3,128,256]{2,1,0:T(8,128)} %get-tuple-element.168), channel_id=1, source_target_pairs={{0,3},{1,2},{2,1},{3,0},{4,7},{5,6},{6,5},{7,4},{8,11},{9,10},{10,... | collective-permute-start | bytes 1179656 | tf_op jit(solution)/shard_map/ppermute | solution.py:36
  265.3 44.3 %collective-permute-start.56 = (f32[3,128,256]{2,1,0:T(8,128)}, f32[3,128,256]{2,1,0:T(8,128)S(1)}, u32[]{:S(2)}, u32[]{:S(2)}) collective-permute-start(f32[3,128,256]{2,1,0:T(8,128)} %get-tuple-element.169), channel_id=1, source_target_pairs={{0,4},{1,5},{2,6},{3,7},{4,0},{5,1},{6,2},{7,3},{8,12},{9,13},{10,... | collective-permute-start | bytes 1179656 | tf_op jit(solution)/shard_map/ppermute | solution.py:36
  272.2 44.9 %collective-permute-start.57 = (f32[3,128,256]{2,1,0:T(8,128)}, f32[3,128,256]{2,1,0:T(8,128)S(1)}, u32[]{:S(2)}, u32[]{:S(2)}) collective-permute-start(f32[3,128,256]{2,1,0:T(8,128)} %get-tuple-element.170), channel_id=1, source_target_pairs={{0,5},{1,4},{2,7},{3,6},{4,1},{5,0},{6,3},{7,2},{8,13},{9,12},{10,... | collective-permute-start | bytes 1179656 | tf_op jit(solution)/shard_map/ppermute | solution.py:36
  273.9 52.8 %collective-permute-start.58 = (f32[3,128,256]{2,1,0:T(8,128)}, f32[3,128,256]{2,1,0:T(8,128)S(1)}, u32[]{:S(2)}, u32[]{:S(2)}) collective-permute-start(f32[3,128,256]{2,1,0:T(8,128)} %get-tuple-element.171), channel_id=1, source_target_pairs={{0,6},{1,7},{2,4},{3,5},{4,2},{5,3},{6,0},{7,1},{8,14},{9,15},{10,... | collective-permute-start | bytes 1179656 | tf_op jit(solution)/shard_map/ppermute | solution.py:36
  287.6 48.1 %collective-permute-start.59 = (f32[3,128,256]{2,1,0:T(8,128)}, f32[3,128,256]{2,1,0:T(8,128)}, u32[]{:S(2)}, u32[]{:S(2)}) collective-permute-start(f32[3,128,256]{2,1,0:T(8,128)} %get-tuple-element.172), channel_id=1, source_target_pairs={{0,7},{1,6},{2,5},{3,4},{4,3},{5,2},{6,1},{7,0},{8,15},{9,14},{10,... | collective-permute-start | bytes 1179656 | tf_op jit(solution)/shard_map/ppermute | solution.py:36
  310.4 52.6 %collective-permute-start.36 = (f32[2,256,256]{2,1,0:T(8,128)}, f32[2,256,256]{2,1,0:T(8,128)S(1)}, u32[]{:S(2)}, u32[]{:S(2)}) collective-permute-start(f32[2,256,256]{2,1,0:T(8,128)} %get-tuple-element.148), channel_id=1, source_target_pairs={{0,8},{8,0},{16,24},{24,16},{1,9},{9,1},{17,25},{25,17},{2,10},{10... | collective-permute-start | bytes 1572872 | tf_op jit(solution)/shard_map/ppermute | solution.py:36
  317.8 46.1 %collective-permute-start.37 = (f32[2,256,256]{2,1,0:T(8,128)}, f32[2,256,256]{2,1,0:T(8,128)S(1)}, u32[]{:S(2)}, u32[]{:S(2)}) collective-permute-start(f32[2,256,256]{2,1,0:T(8,128)} %get-tuple-element.149), channel_id=1, source_target_pairs={{0,16},{8,24},{16,0},{24,8},{1,17},{9,25},{17,1},{25,9},{2,18},{10... | collective-permute-start | bytes 1572872 | tf_op jit(solution)/shard_map/ppermute | solution.py:36
  327.4 37.8 %collective-permute-start.38 = (f32[2,256,256]{2,1,0:T(8,128)}, f32[2,256,256]{2,1,0:T(8,128)S(1)}, u32[]{:S(2)}, u32[]{:S(2)}) collective-permute-start(f32[2,256,256]{2,1,0:T(8,128)} %get-tuple-element.150), channel_id=1, source_target_pairs={{0,24},{8,16},{16,8},{24,0},{1,25},{9,17},{17,9},{25,1},{2,26},{10... | collective-permute-start | bytes 1572872 | tf_op jit(solution)/shard_map/ppermute | solution.py:36
  349.6 40.5 %collective-permute-start.46 = (f32[3,128,256]{2,1,0:T(8,128)}, f32[3,128,256]{2,1,0:T(8,128)S(1)}, u32[]{:S(2)}, u32[]{:S(2)}) collective-permute-start(f32[3,128,256]{2,1,0:T(8,128)} %get-tuple-element.159), channel_id=1, source_target_pairs={{0,1},{1,0},{2,3},{3,2},{4,5},{5,4},{6,7},{7,6},{8,9},{9,8},{10,11... | collective-permute-start | bytes 1179656 | tf_op jit(solution)/shard_map/ppermute | solution.py:36
  390.2 43.3 %collective-permute-start.51 = (f32[3,128,256]{2,1,0:T(8,128)}, f32[3,128,256]{2,1,0:T(8,128)}, u32[]{:S(2)}, u32[]{:S(2)}) collective-permute-start(f32[3,128,256]{2,1,0:T(8,128)} %get-tuple-element.164), channel_id=1, source_target_pairs={{0,6},{1,7},{2,4},{3,5},{4,2},{5,3},{6,0},{7,1},{8,14},{9,15},{10,... | collective-permute-start | bytes 1179656 | tf_op jit(solution)/shard_map/ppermute | solution.py:36
  390.9 57.2 %collective-permute-start.52 = (f32[3,128,256]{2,1,0:T(8,128)}, f32[3,128,256]{2,1,0:T(8,128)}, u32[]{:S(2)}, u32[]{:S(2)}) collective-permute-start(f32[3,128,256]{2,1,0:T(8,128)} %get-tuple-element.165), channel_id=1, source_target_pairs={{0,7},{1,6},{2,5},{3,4},{4,3},{5,2},{6,1},{7,0},{8,15},{9,14},{10,... | collective-permute-start | bytes 1179656 | tf_op jit(solution)/shard_map/ppermute | solution.py:36
  399.7 48.4 %collective-permute-start.39 = (f32[2,128,256]{2,1,0:T(8,128)}, f32[2,128,256]{2,1,0:T(8,128)S(1)}, u32[]{:S(2)}, u32[]{:S(2)}) collective-permute-start(f32[2,128,256]{2,1,0:T(8,128)} %get-tuple-element.152), channel_id=1, source_target_pairs={{0,1},{1,0},{2,3},{3,2},{4,5},{5,4},{6,7},{7,6},{8,9},{9,8},{10,11... | collective-permute-start | bytes 786440 | tf_op jit(solution)/shard_map/ppermute | solution.py:36
  401.1 48.3 %collective-permute-start.40 = (f32[2,128,256]{2,1,0:T(8,128)}, f32[2,128,256]{2,1,0:T(8,128)S(1)}, u32[]{:S(2)}, u32[]{:S(2)}) collective-permute-start(f32[2,128,256]{2,1,0:T(8,128)} %get-tuple-element.153), channel_id=1, source_target_pairs={{0,2},{1,3},{2,0},{3,1},{4,6},{5,7},{6,4},{7,5},{8,10},{9,11},{10,... | collective-permute-start | bytes 786440 | tf_op jit(solution)/shard_map/ppermute | solution.py:36
  448.2 44.5 %collective-permute-start.44 = (f32[2,128,256]{2,1,0:T(8,128)}, f32[2,128,256]{2,1,0:T(8,128)S(1)}, u32[]{:S(2)}, u32[]{:S(2)}) collective-permute-start(f32[2,128,256]{2,1,0:T(8,128)} %get-tuple-element.157), channel_id=1, source_target_pairs={{0,6},{1,7},{2,4},{3,5},{4,2},{5,3},{6,0},{7,1},{8,14},{9,15},{10,... | collective-permute-start | bytes 786440 | tf_op jit(solution)/shard_map/ppermute | solution.py:36
  449.4 49.4 %collective-permute-start.45 = (f32[2,128,256]{2,1,0:T(8,128)}, f32[2,128,256]{2,1,0:T(8,128)}, u32[]{:S(2)}, u32[]{:S(2)}) collective-permute-start(f32[2,128,256]{2,1,0:T(8,128)} %get-tuple-element.158), channel_id=1, source_target_pairs={{0,7},{1,6},{2,5},{3,4},{4,3},{5,2},{6,1},{7,0},{8,15},{9,14},{10,... | collective-permute-start | bytes 786440 | tf_op jit(solution)/shard_map/ppermute | solution.py:36
  450.8 107.9 %collective-permute-start.31 = (f32[1,128,256]{2,1,0:T(8,128)}, f32[1,128,256]{2,1,0:T(8,128)}, u32[]{:S(2)}, u32[]{:S(2)}) collective-permute-start(f32[1,128,256]{2,1,0:T(8,128)} %get-tuple-element.142), channel_id=1, source_target_pairs={{0,3},{1,2},{2,1},{3,0},{4,7},{5,6},{6,5},{7,4},{8,11},{9,10},{10,... | collective-permute-start | bytes 393224 | tf_op jit(solution)/shard_map/ppermute | solution.py:36
  468.3 90.4 %collective-permute-start.32 = (f32[1,128,256]{2,1,0:T(8,128)}, f32[1,128,256]{2,1,0:T(8,128)}, u32[]{:S(2)}, u32[]{:S(2)}) collective-permute-start(f32[1,128,256]{2,1,0:T(8,128)} %get-tuple-element.143), channel_id=1, source_target_pairs={{0,4},{1,5},{2,6},{3,7},{4,0},{5,1},{6,2},{7,3},{8,12},{9,13},{10,... | collective-permute-start | bytes 393224 | tf_op jit(solution)/shard_map/ppermute | solution.py:36
  477.1 81.6 %collective-permute-start.33 = (f32[1,128,256]{2,1,0:T(8,128)}, f32[1,128,256]{2,1,0:T(8,128)}, u32[]{:S(2)}, u32[]{:S(2)}) collective-permute-start(f32[1,128,256]{2,1,0:T(8,128)} %get-tuple-element.144), channel_id=1, source_target_pairs={{0,5},{1,4},{2,7},{3,6},{4,1},{5,0},{6,3},{7,2},{8,13},{9,12},{10,... | collective-permute-start | bytes 393224 | tf_op jit(solution)/shard_map/ppermute | solution.py:36
  492.7 66.0 %collective-permute-start.34 = (f32[1,128,256]{2,1,0:T(8,128)}, f32[1,128,256]{2,1,0:T(8,128)}, u32[]{:S(2)}, u32[]{:S(2)}) collective-permute-start(f32[1,128,256]{2,1,0:T(8,128)} %get-tuple-element.145), channel_id=1, source_target_pairs={{0,6},{1,7},{2,4},{3,5},{4,2},{5,3},{6,0},{7,1},{8,14},{9,15},{10,... | collective-permute-start | bytes 393224 | tf_op jit(solution)/shard_map/ppermute | solution.py:36
  498.8 60.0 %collective-permute-start.35 = (f32[1,128,256]{2,1,0:T(8,128)}, f32[1,128,256]{2,1,0:T(8,128)}, u32[]{:S(2)}, u32[]{:S(2)}) collective-permute-start(f32[1,128,256]{2,1,0:T(8,128)} %get-tuple-element.146), channel_id=1, source_target_pairs={{0,7},{1,6},{2,5},{3,4},{4,3},{5,2},{6,1},{7,0},{8,15},{9,14},{10,... | collective-permute-start | bytes 393224 | tf_op jit(solution)/shard_map/ppermute | solution.py:36
  (116 other events, 2897.4 us)
